TPU v7x, 256 devices: a whole 4x4x8 slice. The times are simulated.
256 devices in a mesh: dp: 16 (over x_lo, z), shard: 16 (over x_hi, y, core).
Axes of the slice: x: 4 (x_hi: 2, x_lo: 2; x = x_hi * 2 + x_lo), y: 4, z: 8, core: 2. Of those that a mesh axis runs over, the one named last changes fastest.
Arguments:
- gradient: bfloat16 [16, 2560, 2560], P(None, ('shard', 'dp')), may hold values from -1.5 to 1.5
- owner: int32 [16], replicated, may hold values from 0 to 15, each once
- a_inverse: bfloat16 [16, 2560, 2560], P('dp', 'shard'), as said below
- b_inverse: bfloat16 [16, 2560, 2560], P('dp', 'shard'), as said below
Outputs:
- preconditioned: bfloat16 [16, 2560, 2560], P(None, ('shard', 'dp'))
Inputs may be any that keep to these rules, and one draw needn't show every extreme that they name: owner names each of the 16 slots for exactly one layer. Every slot of a_inverse is a symmetric matrix. Every slot of b_inverse is a symmetric matrix.
All inputs are finite; a program needn't handle non-finite values.
Results may differ from a plain program's by a relative error of at most 0.0049.
Values may be sent and summed in bfloat16 or wider, within the bound.
No kernel may reach another device: no remote copies, remote signals or barrier semaphores. Data moves between devices by JAX's collectives and lax.ppermute only.
A program may use at most 128 MiB of HBM per device.

v0:
```python
import jax
import jax.numpy as jnp
from jax import lax
from jax.sharding import PartitionSpec as P


def local(gradient, owner, a_inverse, b_inverse):
    layer_count = gradient.shape[0]
    chosen = (owner[:, None] == jnp.arange(layer_count, dtype=jnp.int32)[None, :]).astype(
        jnp.bfloat16
    )
    outgoing = jnp.einsum(
        "lo,lrc->orc", chosen, gradient, preferred_element_type=jnp.float32
    ).astype(jnp.bfloat16)
    owned = lax.all_to_all(outgoing, "dp", split_axis=0, concat_axis=1, tiled=True)
    grad_rows = owned[0]
    right_rows = b_inverse[0]
    left_rows = a_inverse[0]
    columns = grad_rows
    right_half = jnp.dot(
        columns,
        lax.all_gather(right_rows, "shard", axis=0, tiled=True),
        preferred_element_type=jnp.float32,
    ).astype(jnp.bfloat16)
    columns = left_rows
    summed = jnp.dot(
        columns,
        lax.all_gather(right_half, "shard", axis=0, tiled=True),
        preferred_element_type=jnp.float32,
    )
    result_rows = summed.astype(jnp.bfloat16)
    returned = lax.all_to_all(
        result_rows[None, :, :], "dp", split_axis=1, concat_axis=0, tiled=True
    )
    return jnp.take(returned, owner, axis=0)


def solution(mesh):
    in_specs = (P(None, ("shard", "dp"), None), P(), P("dp", "shard", None), P("dp", "shard", None))
    out_specs = P(None, ("shard", "dp"), None)
    return jax.shard_map(local, mesh=mesh, in_specs=in_specs, out_specs=out_specs, check_vma=False)
```

profile of v0, /device:TPU:32, one launch (start us, length us, event | category | flops | bytes accessed | tf_op | source)
XLA Modules:
  0.0 281.3 jit_solution(5845131515558374198)
XLA Ops:
  6.5 0.0 copy-start
  6.5 0.0 all-gather.6.cloned.1.call-start
  6.5 0.7 all-gather.6.cloned.1.call-update
  7.3 0.0 all-gather.4.cloned.1.call-start
  7.3 0.4 copy-done
  7.7 1.0 convolution_convert_fusion.1
  8.7 0.5 copy.7
  9.2 42.1 %all_to_all.21 = bf16[16,10,2560]{2,1,0:T(8,128)(2,1)S(1)} all-to-all(bf16[16,10,2560]{2,1,0:T(8,128)(2,1)S(1)} %copy.7), channel_id=1, replica_groups=mesh['dp'=16,'shard'=16] {'dp'}, dimensions={0} | all-to-all | bytes 1638400 | tf_op jit(solution)/shard_map/all_to_all | solution.py:15
  51.3 0.3 squeeze.9
  51.6 0.0 copy-start.2
  51.6 66.0 %all-gather.6.cloned.1.call-done = bf16[1,2560,2560]{2,1,0:T(8,128)(2,1)} async-done(((bf16[1,160,2560]{2,1,0:T(8,128)(2,1)}), bf16[1,2560,2560]{2,1,0:T(8,128)(2,1)}) %all-gather.6.cloned.1.call-update) | async-done | bytes 13107216 | tf_op jit(solution)/shard_map/all_gather | solution.py:22
  117.6 7.9 %fusion.2 = bf16[160,2560]{1,0:T(8,128)(2,1)} fusion(bf16[160,2560]{1,0:T(8,128)(2,1)S(1)} %squeeze.9, bf16[1,2560,2560]{2,1,0:T(8,128)(2,1)} %all-gather.6.cloned.1.call-done), kind=kOutput, calls=%fused_computation.3 | convolution fusion | flops 2097561600 | bytes 14745600 | tf_op jit(solution)/shard_map/dot_general | solution.py:20
  125.5 0.0 all-gather.4.cloned.1.call-update
  125.5 95.9 %all-gather.4.cloned.1.call-done = bf16[2560,2560]{1,0:T(8,128)(2,1)} async-done(((bf16[160,2560]{1,0:T(8,128)(2,1)}), bf16[2560,2560]{1,0:T(8,128)(2,1)}) %all-gather.4.cloned.1.call-update) | async-done | bytes 13107216 | tf_op jit(solution)/shard_map/all_gather | solution.py:28
  221.5 0.0 copy-done.2
  221.5 7.0 %fusion.5 = bf16[1,160,2560]{2,1,0:T(8,128)(2,1)S(1)} fusion(bf16[2560,2560]{1,0:T(8,128)(2,1)} %all-gather.4.cloned.1.call-done, bf16[1,160,2560]{2,1,0:T(8,128)(2,1)S(1)} %copy-done.2), kind=kOutput, calls=%fused_computation.6 | convolution fusion | flops 2097561600 | bytes 14745600 | tf_op jit(solution)/shard_map/dot_general | solution.py:26
  228.5 1.3 copy.12
  229.8 0.5 broadcast.17
  230.3 5.6 %reduce.2 = bf16[160,2560]{1,0:T(8,128)(2,1)S(1)} reduce(bf16[160,1,2560]{2,1,0:T(2,128)(2,1)S(1)} %bitcast.23, bf16[]{:T(256)} %broadcast.17), dimensions={1}, to_apply=%bitcast.22.reduce_sub_computation | reduce | bytes 1638402
  235.9 0.0 copy-start.1
  235.9 1.3 reshape.25
  237.2 7.5 %all-to-all-start.1 = ((bf16[16,2,12800]{2,1,0:T(2,128)(2,1)}), bf16[16,2,12800]{2,1,0:T(2,128)(2,1)S(1)}, u32[]{:S(2)}, u32[]{:S(2)}) async-start(bf16[16,2,12800]{2,1,0:T(2,128)(2,1)} %reshape.25), calls=%async_computation.1 | async-start | bytes 1638400 | tf_op jit(solution)/shard_map/all_to_all | solution.py:32
  244.7 0.0 copy-done.1
  244.7 21.8 %all-to-all-done.1 = bf16[16,2,12800]{2,1,0:T(2,128)(2,1)S(1)} async-done(((bf16[16,2,12800]{2,1,0:T(2,128)(2,1)}), bf16[16,2,12800]{2,1,0:T(2,128)(2,1)S(1)}, u32[]{:S(2)}, u32[]{:S(2)}) %all-to-all-start.1) | async-done | bytes 819232 | tf_op jit(solution)/shard_map/all_to_all | solution.py:32
  266.6 0.7 reshape.26
  267.2 4.7 %bitcast_reduce_fusion = bf16[160,2560]{1,0:T(8,128)(2,1)S(1)} fusion(bf16[160,1,2560]{2,1,0:T(2,128)(2,1)S(1)} %reshape.26), kind=kLoop, calls=%fused_computation.15 | loop fusion | bytes 1638400 | tf_op jit(solution)/shard_map/all_to_all | solution.py:32
  271.9 0.3 all_to_all.8
  272.3 0.6 gather_fusion
  272.9 0.2 broadcast_select_fusion
  273.1 1.3 copy.9
  (3 shorter events, 0.0 us)
Async XLA Ops:
  6.5 1.1 copy-start
  6.5 111.1 %all-gather.6.cloned.1.call-start = ((), (), s32[]{:S(2)}) async-start(), calls=%async_computation.3 | async-start | bytes 13926400 | tf_op jit(solution)/shard_map/all_gather | solution.py:22
  7.3 214.2 %all-gather.4.cloned.1.call-start = ((), (), s32[]{:S(2)}) async-start(), calls=%async_computation.2 | async-start | bytes 13926400 | tf_op jit(solution)/shard_map/all_gather | solution.py:28
  51.6 169.9 %copy-start.2 = (bf16[1,160,2560]{2,1,0:T(8,128)(2,1)S(1)}, bf16[1,160,2560]{2,1,0:T(8,128)(2,1)}, u32[]{:S(2)}) copy-start(bf16[1,160,2560]{2,1,0:T(8,128)(2,1)} %param.6) | copy-start | bytes 2457604
  235.9 8.8 %copy-start.1 = (s32[16]{0:T(128)S(1)}, s32[16]{0:T(128)}, u32[]{:S(2)}) copy-start(s32[16]{0:T(128)} %param.5) | copy-start | bytes 196
  237.2 29.4 %all-to-all-start.1 = ((bf16[16,2,12800]{2,1,0:T(2,128)(2,1)}), bf16[16,2,12800]{2,1,0:T(2,128)(2,1)S(1)}, u32[]{:S(2)}, u32[]{:S(2)}) async-start(bf16[16,2,12800]{2,1,0:T(2,128)(2,1)} %reshape.25), calls=%async_computation.1 | async-start | bytes 1638400 | tf_op jit(solution)/shard_map/all_to_all | solution.py:32
Sparse Core Ops, SparseCore 0:
  10.1 107.4 all-gather.5
  125.7 95.7 all-gather.3
where the time goes:
time: 282 us; the launch traced here: 281 us
  waiting for transfers between devices  185 us (66%)
  blocking collectives  42.1 us (15%)
  matrix products  15.9 us (6%)
  between operations  13.5 us (5%)
  local copies, waits for them, and re-layouts  11.9 us (4%)
  starting transfers between devices  7.54 us (3%)
  other arithmetic  5.81 us (2%)
    all_gather x1, waiting for transfers between devices, local(): lax.all_gather(right_half, 'shard', axis=0, tiled=True)  95.9 us
    all_gather x1, waiting for transfers between devices, local(): lax.all_gather(right_rows, 'shard', axis=0, tiled=True)  66 us
    all_to_all x1, blocking collectives, local(): lax.all_to_all(outgoing, 'dp', split_axis=0, concat_axis=1, tiled=True)  42.1 us
    all_to_all x1, waiting for transfers between devices, local(): lax.all_to_all(result_rows[None, :, :], 'dp', split_axis=1, concat_axis=0...  21.8 us
    dot_general x1, matrix products, local(): jnp.dot(columns, lax.all_gather(right_rows, 'shard', axis=0, tiled=True),...  7.9 us
    all_to_all x1, starting transfers between devices, local(): lax.all_to_all(result_rows[None, :, :], 'dp', split_axis=1, concat_axis=0...  7.5 us
    dot_general x1, matrix products, local(): jnp.dot(columns, lax.all_gather(right_half, 'shard', axis=0, tiled=True),...  7 us
  transfers between devices with their start and end apart: 3, of which 3 were waited for; matrix products, arithmetic and copies ran while one was open for 1% of the time, Pallas kernels for 0%

commit v1 on v0

--- a/solution.py
+++ b/solution.py
@@ -25,7 +25,9 @@
     columns = left_rows
     summed = jnp.dot(
         columns,
-        lax.all_gather(right_half, "shard", axis=0, tiled=True),
+        jnp.concatenate(
+            lax.all_to_all(jnp.stack([right_half] * lax.axis_size("shard")), "shard", 0, 0), axis=0
+        ),
         preferred_element_type=jnp.float32,
     )
     result_rows = summed.astype(jnp.bfloat16)

time: 282 us -> 336 us (1.19)
  blocking collectives: 42.1 us -> 193 us
  waiting for transfers between devices: 185 us -> 87.7 us
  local copies, waits for them, and re-layouts: 11.9 us -> 17.8 us
  matrix products: 15.9 us -> 10.3 us
    all_to_all x0 -> x1, blocking collectives: none -> 151 us  [local(): lax.all_to_all(jnp.stack([right_half] * lax.axis_size('shard')), 'shard',...]
    all_gather x1 -> x0, waiting for transfers between devices: 95.9 us -> none  [local(): lax.all_gather(right_half, 'shard', axis=0, tiled=True)]
    another operation x0 -> x1, local copies, waits for them, and re-layouts: none -> 5.93 us  [local(): jnp.stack([right_half] * lax.axis_size('shard'))]
    dot_general x1, matrix products: 7 us -> 2.28 us  [local(): jnp.dot(columns, jnp.concatenate(lax.all_to_all(jnp.stack([right_half] *...]
  transfers between devices with their start and end apart: 3 -> 2, of which waited for: 3 -> 2; matrix products, arithmetic and copies ran while one was open for 1% -> 1% of each run, Pallas kernels for 0% -> 0%
where the time goes in v1:
time: 336 us
  blocking collectives  193 us (57%)
  waiting for transfers between devices  87.7 us (26%)
  local copies, waits for them, and re-layouts  17.8 us (5%)
  between operations  13.5 us (4%)
  matrix products  10.3 us (3%)
  starting transfers between devices  7.51 us (2%)
  other arithmetic  5.81 us (2%)
    all_to_all x1, blocking collectives, local(): lax.all_to_all(jnp.stack([right_half] * lax.axis_size('shard')), 'shard',...  151 us
    all_gather x1, waiting for transfers between devices, local(): lax.all_gather(right_rows, 'shard', axis=0, tiled=True)  66 us
    all_to_all x1, blocking collectives, local(): lax.all_to_all(outgoing, 'dp', split_axis=0, concat_axis=1, tiled=True)  42.1 us
    all_to_all x1, waiting for transfers between devices, local(): lax.all_to_all(result_rows[None, :, :], 'dp', split_axis=1, concat_axis=0...  20.9 us
    all_to_all x1, starting transfers between devices, local(): lax.all_to_all(result_rows[None, :, :], 'dp', split_axis=1, concat_axis=0...  7.51 us
    dot_general x1, matrix products, local(): jnp.dot(columns, lax.all_gather(right_rows, 'shard', axis=0, tiled=True),...  7 us
  transfers between devices with their start and end apart: 2, of which 2 were waited for; matrix products, arithmetic and copies ran while one was open for 1% of the time, Pallas kernels for 0%

profile of v1, /device:TPU:32, one launch (start us, length us, event | category | flops | bytes accessed | tf_op | source)
XLA Modules:
  0.0 335.9 jit_solution(12136196975475946362)
XLA Ops:
  6.5 0.0 copy-start
  6.5 0.0 all-gather.3.cloned.1.call-start
  6.5 0.7 all-gather.3.cloned.1.call-update
  7.3 0.4 copy-done
  7.7 1.0 convolution_convert_fusion.1
  8.7 0.5 copy.7
  9.2 42.1 %all_to_all.26 = bf16[16,10,2560]{2,1,0:T(8,128)(2,1)S(1)} all-to-all(bf16[16,10,2560]{2,1,0:T(8,128)(2,1)S(1)} %copy.7), channel_id=1, replica_groups=mesh['dp'=16,'shard'=16] {'dp'}, dimensions={0} | all-to-all | bytes 1638400 | tf_op jit(solution)/shard_map/all_to_all | solution.py:15
  51.3 0.3 squeeze.9
  51.6 66.0 %all-gather.3.cloned.1.call-done = bf16[1,2560,2560]{2,1,0:T(8,128)(2,1)} async-done(((bf16[1,160,2560]{2,1,0:T(8,128)(2,1)}), bf16[1,2560,2560]{2,1,0:T(8,128)(2,1)}) %all-gather.3.cloned.1.call-update) | async-done | bytes 13107216 | tf_op jit(solution)/shard_map/all_gather | solution.py:22
  117.6 7.0 %fusion.2 = bf16[160,2560]{1,0:T(8,128)(2,1)S(1)} fusion(bf16[160,2560]{1,0:T(8,128)(2,1)S(1)} %squeeze.9, bf16[1,2560,2560]{2,1,0:T(8,128)(2,1)} %all-gather.3.cloned.1.call-done), kind=kOutput, calls=%fused_computation.3 | convolution fusion | flops 2097561600 | bytes 14745600 | tf_op jit(solution)/shard_map/dot_general | solution.py:20
  124.6 5.9 %stack.2 = bf16[16,160,2560]{2,1,0:T(8,128)(2,1)} broadcast(bf16[160,2560]{1,0:T(8,128)(2,1)S(1)} %fusion.2), dimensions={1,2} | broadcast | bytes 13926400 | tf_op jit(solution)/shard_map/stack | solution.py:29
  130.6 0.0 copy-start.2
  130.6 151.2 %all_to_all.27 = bf16[16,160,2560]{2,1,0:T(8,128)(2,1)S(1)} all-to-all(bf16[16,160,2560]{2,1,0:T(8,128)(2,1)} %stack.2), channel_id=1, replica_groups=mesh['dp'=16,'shard'=16] {'shard'}, dimensions={0} | all-to-all | bytes 26214400 | tf_op jit(solution)/shard_map/all_to_all | solution.py:29
  281.8 0.0 copy-done.2
  281.8 2.3 fusion.5
  284.1 1.3 copy.12
  285.4 0.5 broadcast.19
  285.9 5.6 %reduce.2 = bf16[160,2560]{1,0:T(8,128)(2,1)S(1)} reduce(bf16[160,1,2560]{2,1,0:T(2,128)(2,1)S(1)} %bitcast.25, bf16[]{:T(256)} %broadcast.19), dimensions={1}, to_apply=%bitcast.23.reduce_sub_computation | reduce | bytes 1638402
  291.5 0.0 copy-start.1
  291.5 1.3 reshape.31
  292.8 7.5 %all-to-all-start.2 = ((bf16[16,2,12800]{2,1,0:T(2,128)(2,1)}), bf16[16,2,12800]{2,1,0:T(2,128)(2,1)S(1)}, u32[]{:S(2)}, u32[]{:S(2)}) async-start(bf16[16,2,12800]{2,1,0:T(2,128)(2,1)} %reshape.31), calls=%async_computation.2 | async-start | bytes 1638400 | tf_op jit(solution)/shard_map/all_to_all | solution.py:34
  300.3 0.0 copy-done.1
  300.3 20.9 %all-to-all-done.2 = bf16[16,2,12800]{2,1,0:T(2,128)(2,1)S(1)} async-done(((bf16[16,2,12800]{2,1,0:T(2,128)(2,1)}), bf16[16,2,12800]{2,1,0:T(2,128)(2,1)S(1)}, u32[]{:S(2)}, u32[]{:S(2)}) %all-to-all-start.2) | async-done | bytes 819232 | tf_op jit(solution)/shard_map/all_to_all | solution.py:34
  321.2 0.7 reshape.32
  321.9 4.7 %bitcast_reduce_fusion = bf16[160,2560]{1,0:T(8,128)(2,1)S(1)} fusion(bf16[160,1,2560]{2,1,0:T(2,128)(2,1)S(1)} %reshape.32), kind=kLoop, calls=%fused_computation.15 | loop fusion | bytes 1638400 | tf_op jit(solution)/shard_map/all_to_all | solution.py:34
  326.6 0.3 all_to_all.22
  326.9 0.6 gather_fusion
  327.6 0.2 broadcast_select_fusion
  327.8 1.3 copy.9
  (3 shorter events, 0.0 us)
Async XLA Ops:
  6.5 1.1 copy-start
  6.5 111.1 %all-gather.3.cloned.1.call-start = ((), (), s32[]{:S(2)}) async-start(), calls=%async_computation.3 | async-start | bytes 13926400 | tf_op jit(solution)/shard_map/all_gather | solution.py:22
  130.6 151.2 %copy-start.2 = (bf16[1,160,2560]{2,1,0:T(8,128)(2,1)S(1)}, bf16[1,160,2560]{2,1,0:T(8,128)(2,1)}, u32[]{:S(2)}) copy-start(bf16[1,160,2560]{2,1,0:T(8,128)(2,1)} %param.6) | copy-start | bytes 2457604
  291.5 8.8 %copy-start.1 = (s32[16]{0:T(128)S(1)}, s32[16]{0:T(128)}, u32[]{:S(2)}) copy-start(s32[16]{0:T(128)} %param.5) | copy-start | bytes 196
  292.8 28.5 %all-to-all-start.2 = ((bf16[16,2,12800]{2,1,0:T(2,128)(2,1)}), bf16[16,2,12800]{2,1,0:T(2,128)(2,1)S(1)}, u32[]{:S(2)}, u32[]{:S(2)}) async-start(bf16[16,2,12800]{2,1,0:T(2,128)(2,1)} %reshape.31), calls=%async_computation.2 | async-start | bytes 1638400 | tf_op jit(solution)/shard_map/all_to_all | solution.py:34
Sparse Core Ops, SparseCore 0:
  10.1 107.4 all-gather.2
